TPU v7x, 32 devices: a whole 2x2x4 slice. The times are simulated.
32 devices in a mesh: dp: 4 (over z), ctx: 8 (over y, x, core).
Axes of the slice: x: 2, y: 2, z: 4, core: 2. Of those that a mesh axis runs over, the one named last changes fastest.
Arguments:
- tokens: bfloat16 [4096, 1152], P(('dp', 'ctx')), may hold values from -6 to 6
- in_gain: bfloat16 [1152], P('dp'), may hold values from 0.099609375 to 1.8984375
- query_weight: bfloat16 [1152, 1024], P('dp'), may hold values from -0.1875 to 0.1875
- key_weight: bfloat16 [1152, 256], P('dp'), may hold values from -0.1875 to 0.1875
- value_weight: bfloat16 [1152, 256], P('dp'), may hold values from -0.1875 to 0.1875
- query_gain: bfloat16 [256], P('dp'), may hold values from 0.099609375 to 1.8984375
- key_gain: bfloat16 [256], P('dp'), may hold values from 0.099609375 to 1.8984375
- out_weight: bfloat16 [1024, 1152], P('dp'), may hold values from -0.75 to 0.75
- attn_post_gain: bfloat16 [1152], P('dp'), may hold values from 0.099609375 to 1.8984375
- ffn_pre_gain: bfloat16 [1152], P('dp'), may hold values from 0.099609375 to 1.8984375
- gate_weight: bfloat16 [1152, 6912], P('dp', 'ctx'), may hold values from -0.1875 to 0.1875
- up_weight: bfloat16 [1152, 6912], P('dp', 'ctx'), may hold values from -0.1875 to 0.1875
- down_weight: bfloat16 [1152, 6912], P('dp', 'ctx'), may hold values from -0.078125 to 0.078125
- ffn_post_gain: bfloat16 [1152], P('dp'), may hold values from 0.099609375 to 1.8984375
- cotangent: bfloat16 [4096, 1152], P(('dp', 'ctx')), may hold values from -6 to 6
Outputs:
- block_out: bfloat16 [4096, 1152], P(('dp', 'ctx'))
- input_grad: float32 [4096, 1152], P(('dp', 'ctx'))
- in_gain_grad: float32 [1152], P('dp')
- query_weight_grad: float32 [1152, 1024], P('dp')
- key_weight_grad: float32 [1152, 256], P('dp')
- value_weight_grad: float32 [1152, 256], P('dp')
- query_gain_grad: float32 [256], P('dp')
- key_gain_grad: float32 [256], P('dp')
- out_weight_grad: float32 [1024, 1152], P('dp')
- attn_post_gain_grad: float32 [1152], P('dp')
- ffn_pre_gain_grad: float32 [1152], P('dp')
- gate_weight_grad: float32 [1152, 6912], P('dp', 'ctx')
- up_weight_grad: float32 [1152, 6912], P('dp', 'ctx')
- down_weight_grad: float32 [1152, 6912], P('dp', 'ctx')
- ffn_post_gain_grad: float32 [1152], P('dp')
All inputs are finite; a program needn't handle non-finite values.
Results may differ from a plain program's by a relative error of at most 0.017.
Values may be sent and summed in bfloat16 or wider, within the bound.
A program may use at most 128 MiB of HBM per device.

v0:
```python
import functools
import math

import jax
import jax.numpy as jnp
from jax import lax
from jax.experimental import pallas as pl
from jax.experimental.pallas import tpu as pltpu
from jax.sharding import PartitionSpec as P

HEADS = 4
HEAD = 256


EPS = 1e-06
GELU_C = math.sqrt(2.0 / math.pi)
NEG_FILL = -1e30


def inverse_rms(values):
    return lax.rsqrt(jnp.mean(values * values, axis=-1, keepdims=True) + EPS)


def norm_back(values, scale_inv, gain, grad_out):
    weighted = grad_out * gain
    cubed = scale_inv * scale_inv * scale_inv
    return scale_inv * weighted - values * cubed * jnp.mean(
        weighted * values, axis=-1, keepdims=True
    )


def gelu_pair(values):
    inner = GELU_C * (values + 0.044715 * values * values * values)
    tanh_val = jnp.tanh(inner)
    result = 0.5 * values * (1.0 + tanh_val)
    slope = 0.5 * (1.0 + tanh_val) + 0.5 * values * (1.0 - tanh_val * tanh_val) * GELU_C * (
        1.0 + 3.0 * 0.044715 * values * values
    )
    return (result, slope)


def rotate(values, cosine, sine):
    middle = values.shape[-1] // 2
    first = values[..., :middle]
    second = values[..., middle:]
    return jnp.concatenate(
        [first * cosine - second * sine, second * cosine + first * sine], axis=-1
    )


def unrotate(grads, cosine, sine):
    middle = grads.shape[-1] // 2
    first = grads[..., :middle]
    second = grads[..., middle:]
    return jnp.concatenate(
        [first * cosine + second * sine, second * cosine - first * sine], axis=-1
    )


def rope_tables(positions):
    middle = HEAD // 2
    freqs = jnp.exp(-(2.0 * jnp.arange(middle, dtype=jnp.float32) / HEAD) * math.log(1000000.0))
    angles = positions[:, None] * freqs[None, :]
    return (jnp.cos(angles), jnp.sin(angles))


def matmul(left, right):
    return jnp.dot(left, right, preferred_element_type=jnp.float32)


def matmul_tn(left, right):
    return lax.dot_general(
        left, right, (((0,), (0,)), ((), ())), preferred_element_type=jnp.float32
    )


def matmul_nt(left, right):
    return lax.dot_general(
        left, right, (((1,), (1,)), ((), ())), preferred_element_type=jnp.float32
    )


MESH = pl.DeviceIdType.MESH


def swap_kernel(size, axis, kinds, *refs):
    count = len(kinds)
    ins, outs, kept = refs[:count], refs[count : 2 * count], refs[2 * count : 3 * count]
    send, recv, local = refs[3 * count :]
    me = lax.axis_index(axis)
    own = []
    for item, kind in enumerate(kinds):
        source = ins[item].at[me] if kind == "swap" else ins[item]
        own.append(pltpu.make_async_copy(source, kept[item], local.at[item, 0]))
        own[-1].start()
    barrier = pltpu.get_barrier_semaphore()
    for step in range(1, size):
        peer = lax.rem(me + step, size)
        pl.semaphore_signal(barrier, inc=1, device_id={axis: peer}, device_id_type=MESH)
    pl.semaphore_wait(barrier, size - 1)
    copies = []
    for item, kind in enumerate(kinds):
        for step in range(1, size):
            peer = lax.rem(me + step, size)
            source = ins[item].at[peer] if kind == "swap" else ins[item]
            copy = pltpu.make_async_remote_copy(
                src_ref=source,
                dst_ref=outs[item].at[me],
                send_sem=send.at[item, step - 1],
                recv_sem=recv.at[item, step - 1],
                device_id={axis: peer},
                device_id_type=MESH,
            )
            copy.start()
            copies.append(copy)
    for item in range(count):
        own[item].wait()
        copy = pltpu.make_async_copy(kept[item], outs[item].at[me], local.at[item, 1])
        copy.start()
        copies.append(copy)
    for copy in copies:
        copy.wait()


def chunks_of(rows):
    for parts in (4, 3, 2):
        if rows % (16 * parts) == 0:
            return parts
    return 1


def pair_gather_kernel(size, axis, kinds, *refs):
    count = len(kinds)
    ins, outs, kept = refs[:count], refs[count : 2 * count], refs[2 * count : 3 * count]
    send, recv, pass_send, pass_recv, local = refs[3 * count :]
    me = lax.axis_index(axis)
    twin = me + 1 - 2 * lax.rem(me, 2)
    half = size // 2
    own = []
    for item in range(count):
        own.append(pltpu.make_async_copy(ins[item], kept[item], local.at[item, 0]))
        own[-1].start()
    barrier = pltpu.get_barrier_semaphore()
    for step in range(1, half):
        peer = lax.rem(me + 2 * step, size)
        pl.semaphore_signal(barrier, inc=1, device_id={axis: peer}, device_id_type=MESH)
    pl.semaphore_signal(barrier, inc=1, device_id={axis: twin}, device_id_type=MESH)
    pl.semaphore_wait(barrier, half)
    pieces = []
    for item in range(count):
        rows = ins[item].shape[0]
        pieces += [
            (item, part, pl.ds(part * (rows // chunks_of(rows)), rows // chunks_of(rows)))
            for part in range(chunks_of(rows))
        ]
    across, last = [], []
    for item, part, span in pieces:
        for step in range(1, half):
            copy = pltpu.make_async_remote_copy(
                src_ref=ins[item].at[span],
                dst_ref=outs[item].at[me, span],
                send_sem=send.at[item, step, part],
                recv_sem=recv.at[item, step, part],
                device_id={axis: lax.rem(me + 2 * step, size)},
                device_id_type=MESH,
            )
            copy.start()
            across.append((copy, item, step, part, span))
    for item, part, span in pieces:
        copy = pltpu.make_async_remote_copy(
            src_ref=ins[item].at[span],
            dst_ref=outs[item].at[me, span],
            send_sem=pass_send.at[item, 0, part],
            recv_sem=pass_recv.at[item, 0, part],
            device_id={axis: twin},
            device_id_type=MESH,
        )
        copy.start()
        last.append(copy)
    for item in range(count):
        own[item].wait()
        copy = pltpu.make_async_copy(kept[item], outs[item].at[me], local.at[item, 1])
        copy.start()
        last.append(copy)
    for arrived, item, step, part, span in across:
        arrived.wait_recv()
        origin = lax.rem(me + size - 2 * step, size)
        copy = pltpu.make_async_remote_copy(
            src_ref=outs[item].at[origin, span],
            dst_ref=outs[item].at[origin, span],
            send_sem=pass_send.at[item, step, part],
            recv_sem=pass_recv.at[item, step, part],
            device_id={axis: twin},
            device_id_type=MESH,
        )
        copy.start()
        last.append(copy)
    for sent, *_ in across:
        sent.wait_send()
    for copy in last:
        copy.wait()


def exchange(arrays, kinds, axis, size, ident):
    count = len(arrays)
    pairs = all(kind == "gather" for kind in kinds) and axis == "ctx" and size % 2 == 0
    shapes = tuple(
        jax.ShapeDtypeStruct(x.shape if kind == "swap" else (size,) + x.shape, x.dtype)
        for x, kind in zip(arrays, kinds)
    )
    dma = pltpu.SemaphoreType.DMA
    if pairs:
        half = size // 2
        parts = max(chunks_of(x.shape[0]) for x in arrays)
        scratch = [dma((count, half, parts))] * 4
        body = pair_gather_kernel
    else:
        scratch = [dma((count, size - 1))] * 2
        body = swap_kernel
    moved = sum(x.size * x.dtype.itemsize for x in shapes)
    return pl.pallas_call(
        functools.partial(body, size, axis, tuple(kinds)),
        out_shape=shapes,
        in_specs=[pl.BlockSpec(memory_space=pl.ANY)] * count,
        out_specs=tuple(pl.BlockSpec(memory_space=pl.ANY) for _ in arrays),
        scratch_shapes=[pltpu.VMEM(x.shape[1:], x.dtype) for x in shapes]
        + scratch
        + [dma((count, 2))],
        compiler_params=pltpu.CompilerParams(collective_id=ident, has_side_effects=True),
        cost_estimate=pl.CostEstimate(flops=0, bytes_accessed=20 * moved, transcendentals=0),
        name=f"exchange_{ident}",
    )(*arrays)


def by_columns(array, parts):
    rows, columns = array.shape
    return jnp.transpose(array.reshape(rows, parts, columns // parts), (1, 0, 2))


def from_columns(array):
    parts, rows, columns = array.shape
    return jnp.transpose(array, (1, 0, 2)).reshape(rows, parts * columns)


def sum_blocks(array):
    return jnp.sum(array.astype(jnp.float32), axis=0)


def on_device(
    dp,
    ctx,
    tokens,
    in_gain,
    query_weight,
    key_weight,
    value_weight,
    query_gain,
    key_gain,
    out_weight,
    attn_post_gain,
    ffn_pre_gain,
    gate_weight,
    up_weight,
    down_weight,
    ffn_post_gain,
    cotangent,
):
    rows, width = tokens.shape
    bf16 = jnp.bfloat16
    scaling = 1.0 / math.sqrt(HEAD)
    ctx_index = lax.axis_index("ctx")
    query_pos = ctx_index * rows + jnp.arange(rows, dtype=jnp.int32)
    cosine, sine = rope_tables(query_pos.astype(jnp.float32))

    qwidth = query_weight.shape[1]
    kwidth = key_weight.shape[1]
    mixed_columns = (qwidth + 2 * kwidth) // ctx
    out_columns = out_weight.shape[1] // ctx
    query_columns = qwidth // ctx
    pair = jnp.concatenate([key_weight, value_weight], axis=1)
    pair_rows = pair.shape[0] // ctx
    out_rows = out_weight.shape[0] // ctx
    query_slice = lax.dynamic_slice_in_dim(query_weight, ctx_index * query_columns, query_columns, 1)
    pair_slice = lax.dynamic_slice_in_dim(pair, ctx_index * pair_rows, pair_rows, 0)
    out_slice = lax.dynamic_slice_in_dim(out_weight, ctx_index * out_rows, out_rows, 0)
    gains = (in_gain, query_gain, key_gain, attn_post_gain, ffn_pre_gain, ffn_post_gain)
    cuts = [0]
    for gain in gains:
        cuts.append(cuts[-1] + gain.shape[0])
    packed_gains = jnp.concatenate([gain.astype(jnp.float32) for gain in gains])[None]
    query_dp, pair_dp, out_dp, gains_dp = exchange(
        (query_slice, pair_slice, out_slice, packed_gains), ("gather",) * 4, "dp", dp, 0
    )
    gate_weight, up_weight, down_weight, query_dp = lax.optimization_barrier(
        (gate_weight, up_weight, down_weight, query_dp)
    )
    gate_full, up_full, down_full = (
        lax.all_gather(gate_weight, "dp", axis=0, tiled=True),
        lax.all_gather(up_weight, "dp", axis=0, tiled=True),
        lax.all_gather(down_weight, "dp", axis=0, tiled=True),
    )
    gains_dp = gains_dp[:, 0]
    gain_in, gain_query, gain_key, gain_attn, gain_pre, gain_post = (
        gains_dp[:, low:high].reshape(-1) for low, high in zip(cuts[:-1], cuts[1:])
    )
    query_all, pair_all, out_all, tokens_all = exchange(
        (query_dp.reshape(-1, query_columns), pair_dp, out_dp, tokens),
        ("gather",) * 4,
        "ctx",
        ctx,
        1,
    )
    query_full = from_columns(query_all)
    pair_full = jnp.transpose(pair_all, (1, 0, 2, 3)).reshape(-1, 2 * kwidth)
    key_full = pair_full[:, :kwidth]
    value_full = pair_full[:, kwidth:]
    out_full = jnp.transpose(out_all, (1, 0, 2, 3)).reshape(-1, out_weight.shape[1])

    inputs_f = tokens.astype(jnp.float32)
    inv_one = inverse_rms(inputs_f)
    normed_one = (inputs_f * inv_one * gain_in).astype(bf16)
    all_f = tokens_all.reshape(-1, width).astype(jnp.float32)
    normed_all = (all_f * inverse_rms(all_f) * gain_in).astype(bf16)
    key_pos = jnp.arange(all_f.shape[0], dtype=jnp.int32)
    cosine_all, sine_all = rope_tables(key_pos.astype(jnp.float32))
    queries = matmul(normed_one, query_full).reshape(rows, HEADS, HEAD)
    keys = matmul(normed_one, key_full)
    keys_every = matmul(normed_all, key_full)
    value_all = matmul(normed_all, value_full).astype(bf16)
    inv_query = inverse_rms(queries)
    inv_key = inverse_rms(keys)
    query_rot = (
        rotate(queries * inv_query * gain_query, cosine[:, None, :], sine[:, None, :]) * scaling
    ).astype(bf16)
    key_all = rotate(
        keys_every * inverse_rms(keys_every) * gain_key, cosine_all, sine_all
    ).astype(bf16)
    allowed = (query_pos[:, None] >= key_pos[None, :])[None]
    scores = jnp.einsum("qhd,kd->hqk", query_rot, key_all, preferred_element_type=jnp.float32)
    scores = jnp.where(allowed, scores, NEG_FILL)
    row_max = jnp.max(scores, axis=-1, keepdims=True)
    weights = jnp.where(allowed, jnp.exp(scores - row_max), 0.0)
    total = jnp.sum(weights, axis=-1, keepdims=True)
    accum = jnp.einsum(
        "hqk,kd->hqd", weights.astype(bf16), value_all, preferred_element_type=jnp.float32
    )
    log_total = row_max + jnp.log(total)
    attn_heads = jnp.transpose(accum / total, (1, 0, 2)).astype(bf16)
    attn_out = attn_heads.reshape(rows, HEADS * HEAD)
    projected = matmul(attn_out, out_full)
    inv_proj = inverse_rms(projected)
    residual = inputs_f + projected * inv_proj * gain_attn
    inv_two = inverse_rms(residual)
    normed_two = (residual * inv_two * gain_pre).astype(bf16)

    attn_all = lax.all_gather(attn_out, "ctx", axis=0, tiled=True)
    (rows_all,) = exchange((normed_two,), ("gather",), "ctx", ctx, 2)
    rows_all = rows_all.reshape(-1, width)
    gate = matmul(rows_all, gate_full)
    upper = matmul(rows_all, up_full)
    gelu_val, gelu_der = gelu_pair(gate)
    hidden = (gelu_val * upper).astype(bf16)
    ffn_part = matmul_nt(hidden, down_full).astype(bf16).reshape(ctx, rows, width)
    (ffn_parts,) = exchange((ffn_part,), ("swap",), "ctx", ctx, 3)
    ffn_sum = sum_blocks(ffn_parts)
    inv_ffn = inverse_rms(ffn_sum)
    block_out = (residual + ffn_sum * inv_ffn * gain_post).astype(bf16)
    cot = cotangent.astype(jnp.float32)
    grad_post = jnp.sum(cot * ffn_sum * inv_ffn, axis=0)
    ffn_sum_grad = norm_back(ffn_sum, inv_ffn, gain_post, cot).astype(bf16)

    (grad_all,) = exchange((ffn_sum_grad,), ("gather",), "ctx", ctx, 4)
    grad_all, attn_all = lax.optimization_barrier((grad_all.reshape(-1, width), attn_all))
    down_part, grad_all = lax.optimization_barrier(
        (matmul_tn(grad_all, hidden).astype(bf16), grad_all)
    )
    down_shard = lax.psum_scatter(down_part, "dp", scatter_dimension=0, tiled=True)
    down_shard = down_shard.astype(jnp.float32)
    hidden_grad = matmul(grad_all, down_full)
    gate_grad = (hidden_grad * upper * gelu_der).astype(bf16)
    up_grad = (hidden_grad * gelu_val).astype(bf16)
    two_part, gate_part, up_part = lax.optimization_barrier(
        (
            (matmul_nt(gate_grad, gate_full) + matmul_nt(up_grad, up_full)).astype(bf16),
            matmul_tn(rows_all, gate_grad).astype(bf16),
            matmul_tn(rows_all, up_grad).astype(bf16),
        )
    )
    gate_shard = lax.psum_scatter(gate_part, "dp", scatter_dimension=0, tiled=True)
    gate_shard = gate_shard.astype(jnp.float32)
    up_shard = lax.psum_scatter(up_part, "dp", scatter_dimension=0, tiled=True)
    up_shard = up_shard.astype(jnp.float32)
    (two_parts,) = exchange((two_part.reshape(ctx, rows, width),), ("swap",), "ctx", ctx, 5)
    normed_two_grad = sum_blocks(two_parts)
    grad_pre = jnp.sum(normed_two_grad * residual * inv_two, axis=0)
    residual_grad = cot + norm_back(residual, inv_two, gain_pre, normed_two_grad)
    grad_attn = jnp.sum(residual_grad * projected * inv_proj, axis=0)
    projected_grad = norm_back(projected, inv_proj, gain_attn, residual_grad).astype(bf16)
    attn_out_grad = matmul_nt(projected_grad, out_full).astype(bf16).reshape(rows, HEADS, HEAD)
    delta = jnp.sum(attn_out_grad.astype(jnp.float32) * attn_heads.astype(jnp.float32), axis=-1)
    delta = jnp.transpose(delta, (1, 0))[:, :, None]
    probs = jnp.where(allowed, jnp.exp(scores - log_total), 0.0)
    prob_grad = jnp.einsum(
        "qhd,kd->hqk", attn_out_grad, value_all, preferred_element_type=jnp.float32
    )
    score_grad = (probs * (prob_grad - delta)).astype(bf16)
    values_part = jnp.einsum(
        "hqk,qhd->kd", probs.astype(bf16), attn_out_grad, preferred_element_type=jnp.float32
    )
    keys_part = jnp.einsum("hqk,qhd->kd", score_grad, query_rot, preferred_element_type=jnp.float32)
    query_rot_grad = jnp.einsum(
        "hqk,kd->qhd", score_grad, key_all, preferred_element_type=jnp.float32
    )
    keys_parts, values_parts = exchange(
        (
            keys_part.astype(bf16).reshape(ctx, rows, kwidth),
            values_part.astype(bf16).reshape(ctx, rows, kwidth),
        ),
        ("swap", "swap"),
        "ctx",
        ctx,
        6,
    )
    key_rot_grad = sum_blocks(keys_parts)
    value_grad = sum_blocks(values_parts).astype(bf16)
    query_normed_grad = unrotate(query_rot_grad * scaling, cosine[:, None, :], sine[:, None, :])
    grad_qgain = jnp.sum(query_normed_grad * queries * inv_query, axis=(0, 1))
    query_grad = (
        norm_back(queries, inv_query, gain_query, query_normed_grad)
        .reshape(rows, HEADS * HEAD)
        .astype(bf16)
    )
    key_normed_grad = unrotate(key_rot_grad, cosine, sine)
    grad_kgain = jnp.sum(key_normed_grad * keys * inv_key, axis=0)
    key_grad = norm_back(keys, inv_key, gain_key, key_normed_grad).astype(bf16)
    mixed_grad = jnp.concatenate([query_grad, key_grad, value_grad], axis=1)
    normed_one_grad = matmul_nt(query_grad, query_full) + matmul_nt(
        mixed_grad[:, qwidth:], pair_full
    )
    grad_in = jnp.sum(normed_one_grad * inputs_f * inv_one, axis=0)
    input_grad = residual_grad + norm_back(inputs_f, inv_one, gain_in, normed_one_grad)

    gain_grads = (grad_in, grad_qgain, grad_kgain, grad_attn, grad_pre, grad_post)
    packed = jnp.concatenate([grad.reshape(dp, -1) for grad in gain_grads], axis=1)
    both = jnp.concatenate([by_columns(mixed_grad, ctx), by_columns(projected_grad, ctx)], axis=2)
    both, gain_parts = exchange(
        (both, by_columns(packed, ctx)),
        ("swap",) * 2,
        "ctx",
        ctx,
        7,
    )
    mixed_w = matmul_tn(normed_all, both[:, :, :mixed_columns].reshape(-1, mixed_columns)).astype(bf16)
    out_w = matmul_tn(attn_all, both[:, :, mixed_columns:].reshape(-1, out_columns)).astype(bf16)
    mixed_w, out_w, gain_parts = exchange(
        (
            mixed_w.reshape(dp, -1, mixed_columns),
            out_w.reshape(dp, -1, out_columns),
            sum_blocks(gain_parts)[:, None],
        ),
        ("swap",) * 3,
        "dp",
        dp,
        8,
    )
    mixed_w, out_w, gain_parts = exchange(
        (sum_blocks(mixed_w).astype(bf16), sum_blocks(out_w).astype(bf16), sum_blocks(gain_parts)),
        ("gather",) * 3,
        "ctx",
        ctx,
        9,
    )
    mixed_w = from_columns(mixed_w).astype(jnp.float32)
    out_w = from_columns(out_w).astype(jnp.float32)
    gain_done = gain_parts.reshape(-1)
    share = [gain_done[low:high] for low, high in zip(cuts[:-1], cuts[1:])]
    return (
        block_out,
        input_grad,
        share[0],
        mixed_w[:, :qwidth],
        mixed_w[:, qwidth : qwidth + kwidth],
        mixed_w[:, qwidth + kwidth :],
        share[1],
        share[2],
        out_w,
        share[3],
        share[4],
        gate_shard,
        up_shard,
        down_shard,
        share[5],
    )


def solution(mesh):
    return jax.shard_map(
        functools.partial(on_device, mesh.shape["dp"], mesh.shape["ctx"]),
        mesh=mesh,
        in_specs=(
            P(("dp", "ctx"), None),
            P("dp"),
            P("dp", None),
            P("dp", None),
            P("dp", None),
            P("dp"),
            P("dp"),
            P("dp", None),
            P("dp"),
            P("dp"),
            P("dp", "ctx"),
            P("dp", "ctx"),
            P("dp", "ctx"),
            P("dp"),
            P(("dp", "ctx"), None),
        ),
        out_specs=(
            P(("dp", "ctx"), None),
            P(("dp", "ctx"), None),
            P("dp"),
            P("dp", None),
            P("dp", None),
            P("dp", None),
            P("dp"),
            P("dp"),
            P("dp", None),
            P("dp"),
            P("dp"),
            P("dp", "ctx"),
            P("dp", "ctx"),
            P("dp", "ctx"),
            P("dp"),
        ),
        check_vma=False,
    )
```

profile of v0, /device:TPU:0, one launch (start us, length us, event | category | flops | bytes accessed | tf_op | source)
XLA Modules:
  0.0 481.5 jit_solution(9725981886471831568)
XLA Ops:
  7.3 4.2 concatenate.33
  15.7 23.1 %exchange_0.1 = (bf16[4,288,128]{2,1,0:T(8,128)(2,1)}, bf16[4,36,512]{2,1,0:T(8,128)(2,1)}, bf16[4,32,1152]{2,1,0:T(8,128)(2,1)}, f32[4,1,1280]{2,1,0:T(1,128)}) custom-call(bf16[288,128]{1,0:T(8,128)(2,1)} %constant_dynamic-slice_fusion.1.refs_0_, bf16[36,512]{1,0:T(8,128)(2,1)} %fusion.74.refs_1_, bf16[32,1152]{1,0:T(8,128)(2,1)} %constant_dynamic-slice_fusion.refs_2_, ...), custom_call_target="tpu_custom_call" | custom-call | bytes 15155200 | tf_op jit(solution)/shard_map/exchange_0/pallas_call | solution.py:221
  41.5 52.4 %exchange_1.1 = (bf16[8,1152,128]{2,1,0:T(8,128)(2,1)}, bf16[8,4,36,512]{3,2,1,0:T(8,128)(2,1)}, bf16[8,4,32,1152]{3,2,1,0:T(8,128)(2,1)}, bf16[8,128,1152]{2,1,0:T(8,128)(2,1)}) custom-call(bf16[1152,128]{1,0:T(8,128)(2,1)} %bitcast.177, bf16[4,36,512]{2,1,0:T(8,128)(2,1)} %get-tuple-element.46.refs_1_, bf16[4,32,1152]{2,1,0:T(8,128)(2,1)} %get-tuple-element.47.refs_2_, ...), custom_call_target="tpu_custom_call" | custom-call | bytes 165150720 | tf_op jit(solution)/shard_map/exchange_1/pallas_call | solution.py:221
  101.7 3.8 fusion.1
  128.7 18.8 %exchange_2.1 = bf16[8,128,1152]{2,1,0:T(8,128)(2,1)} custom-call(bf16[128,1152]{1,0:T(8,128)(2,1)} %multiply_convert_fusion.4.refs_0_), custom_call_target="tpu_custom_call" | custom-call | bytes 47185920 | tf_op jit(solution)/shard_map/exchange_2/pallas_call | solution.py:221
  148.2 6.6 %fusion.95 = f32[1024,864]{0,1:T(8,128)} fusion(bf16[1024,1152]{1,0:T(8,128)(2,1)} %bitcast.153, bf16[1152,864]{1,0:T(8,128)(2,1)} %all-gather.5.cloned.1.call-done), kind=kOutput, calls=%fused_computation.198 | convolution fusion | flops 2038431744 | bytes 7888896 | tf_op jit(solution)/shard_map/dot_general | solution.py:68
  154.8 9.0 %multiply_convert_fusion.2 = (bf16[1024,864]{0,1:T(8,128)(2,1)}, f32[1024,864]{0,1:T(8,128)}) fusion(f32[1024,864]{0,1:T(8,128)} %fusion.95, bf16[1024,1152]{1,0:T(8,128)(2,1)} %bitcast.154, bf16[1152,864]{1,0:T(8,128)(2,1)} %all-gather.7.cloned.1.call-done), kind=kOutput, calls=%fused_computation.19 | convolution fusion | flops 2047279104 | bytes 13197312 | tf_op jit(solution)/shard_map/dot_general | solution.py:68
  163.8 11.5 %all-gather.9.cloned.1.call-done = bf16[1152,864]{1,0:T(8,128)(2,1)} async-done(((bf16[288,864]{1,0:T(8,128)(2,1)}), bf16[1152,864]{1,0:T(8,128)(2,1)}) %all-gather.9.cloned.1.call-update) | async-done | bytes 1990672 | tf_op jit(solution)/shard_map/all_gather | solution.py:300
  175.3 6.4 %convolution_convert_fusion = bf16[1024,1152]{1,0:T(8,128)(2,1)} fusion(bf16[1024,864]{0,1:T(8,128)(2,1)} %get-tuple-element.183, bf16[1152,864]{1,0:T(8,128)(2,1)} %all-gather.9.cloned.1.call-done), kind=kOutput, calls=%fused_computation.10 | convolution fusion | flops 2039611392 | bytes 6119424 | tf_op jit(solution)/shard_map/dot_general | solution.py:78
  181.7 36.3 %exchange_3.1 = bf16[8,128,1152]{2,1,0:T(8,128)(2,1)} custom-call(bf16[8,128,1152]{2,1,0:T(8,128)(2,1)} %bitcast.161), custom_call_target="tpu_custom_call" | custom-call | bytes 47185920 | tf_op jit(solution)/shard_map/exchange_3/pallas_call | solution.py:221
  222.2 19.1 %exchange_4.1 = bf16[8,128,1152]{2,1,0:T(8,128)(2,1)} custom-call(bf16[128,1152]{1,0:T(8,128)(2,1)} %get-tuple-element.143.refs_0_), custom_call_target="tpu_custom_call" | custom-call | bytes 47185920 | tf_op jit(solution)/shard_map/exchange_4/pallas_call | solution.py:221
  241.4 6.5 %convolution_convert_fusion.3 = bf16[1152,864]{0,1:T(8,128)(2,1)} fusion(bf16[1024,864]{0,1:T(8,128)(2,1)} %get-tuple-element.183, bf16[1024,1152]{1,0:T(8,128)(2,1)} %bitcast.159), kind=kOutput, calls=%fused_computation.22 | convolution fusion | flops 2039427072 | bytes 6119424 | tf_op jit(solution)/shard_map/dot_general | solution.py:72
  247.9 4.8 %multiply_convert_fusion.1 = (bf16[1024,864]{0,1:T(8,128)(2,1)S(1)}, bf16[1024,864]{0,1:T(8,128)(2,1)S(1)}) fusion(f32[1024,864]{0,1:T(8,128)S(1)} %copy-done.75, f32[1024,864]{0,1:T(8,128)S(1)} %copy-done.76, bf16[1024,1152]{1,0:T(8,128)(2,1)S(1)} %bitcast.160, bf16[1152,864]{1,0:T(8,128)(2,1)S(1)} %copy-done.72), kind=kOutput, calls=%fused_computation.18 | convolution fusion | flops 2058780672 | bytes 14966784 | tf_op jit(solution)/shard_map/dot_general | solution.py:68
  252.7 3.8 convolution_convert_fusion.2
  256.5 3.7 convolution_convert_fusion.1
  263.2 4.3 add_convert_fusion
  267.5 4.1 copy.104
  277.2 27.7 %exchange_5.1 = bf16[8,128,1152]{2,1,0:T(8,128)(2,1)} custom-call(bf16[8,128,1152]{2,1,0:T(8,128)(2,1)} %bitcast.157), custom_call_target="tpu_custom_call" | custom-call | bytes 47185920 | tf_op jit(solution)/shard_map/exchange_5/pallas_call | solution.py:221
  304.9 4.1 copy.106
  319.9 4.1 copy.108
  330.4 16.1 %exchange_6.1 = (bf16[8,128,256]{2,1,0:T(8,128)(2,1)}, bf16[8,128,256]{2,1,0:T(8,128)(2,1)}) custom-call(bf16[8,128,256]{2,1,0:T(8,128)(2,1)} %bitcast.175, bf16[8,128,256]{2,1,0:T(8,128)(2,1)} %bitcast.176), custom_call_target="tpu_custom_call" | custom-call | bytes 20971520 | tf_op jit(solution)/shard_map/exchange_6/pallas_call | solution.py:221
  367.7 13.9 %exchange_7.1 = (bf16[8,128,336]{2,1,0:T(8,128)(2,1)}, f32[8,4,160]{2,1,0:T(4,128)}) custom-call(bf16[8,128,336]{2,1,0:T(8,128)(2,1)} %pad_maximum_fusion.refs_0_, f32[8,4,160]{2,1,0:T(4,128)} %bitcast.178), custom_call_target="tpu_custom_call" | custom-call | bytes 14172160 | tf_op jit(solution)/shard_map/exchange_7/pallas_call | solution.py:221
  392.7 31.7 %exchange_8.1 = (bf16[4,288,192]{2,1,0:T(8,128)(2,1)}, bf16[4,256,144]{2,1,0:T(8,128)(2,1)}, f32[4,1,160]{2,1,0:T(1,128)}) custom-call(bf16[4,288,192]{2,1,0:T(8,128)(2,1)} %bitcast.162, bf16[4,256,144]{2,1,0:T(8,128)(2,1)} %bitcast.167, f32[4,1,160]{2,1,0:T(1,128)} %broadcast_in_dim.33.refs_2_), custom_call_target="tpu_custom_call" | custom-call | bytes 14796800 | tf_op jit(solution)/shard_map/exchange_8/pallas_call | solution.py:221
  429.4 19.0 %exchange_9.1 = (bf16[8,288,192]{2,1,0:T(8,128)(2,1)}, bf16[8,256,144]{2,1,0:T(8,128)(2,1)}, f32[8,1,160]{2,1,0:T(1,128)}) custom-call(bf16[288,192]{1,0:T(8,128)(2,1)} %reduce_sum.308.refs_0_, bf16[256,144]{1,0:T(8,128)(2,1)} %reduce_sum.309.refs_1_, f32[1,160]{1,0:T(1,128)} %bitcast.182), custom_call_target="tpu_custom_call" | custom-call | bytes 29593600 | tf_op jit(solution)/shard_map/exchange_9/pallas_call | solution.py:221
  (301 shorter events, 130.8 us)
Async XLA Ops:
  7.2 34.1 %copy-start.4 = (bf16[128,1152]{1,0:T(8,128)(2,1)S(1)}, bf16[128,1152]{1,0:T(8,128)(2,1)}, u32[]{:S(2)}) copy-start(bf16[128,1152]{1,0:T(8,128)(2,1)} %refs_3_.1) | copy-start | bytes 884740
  7.2 141.0 %all-gather.5.cloned.1.call-start = ((), (), s32[]{:S(2)}) async-start(), calls=%async_computation.3 | async-start | bytes 2580480 | tf_op jit(solution)/shard_map/all_gather | solution.py:298
  38.8 116.0 %all-gather.7.cloned.1.call-start = ((), (), s32[]{:S(2)}) async-start(), calls=%async_computation.4 | async-start | bytes 2580480 | tf_op jit(solution)/shard_map/all_gather | solution.py:299
  39.5 135.8 %all-gather.9.cloned.1.call-start = ((), (), s32[]{:S(2)}) async-start(), calls=%async_computation.5 | async-start | bytes 2580480 | tf_op jit(solution)/shard_map/all_gather | solution.py:300
  40.3 201.0 %all-gather.11.cloned.1.call-start = ((), (), s32[]{:S(2)}) async-start(), calls=%async_computation.6 | async-start | bytes 2359296 | tf_op jit(solution)/shard_map/all_gather | solution.py:356
  40.3 69.7 %copy-start.65 = (f32[128]{0:T(128)}, f32[128]{0:T(128)S(1)}, u32[]{:S(2)}) copy-start(f32[128]{0:T(128)S(1)} %get-tuple-element.189) | copy-start | bytes 1540
  101.7 8.7 %copy-start.50 = (f32[256]{0:T(256)}, f32[256]{0:T(256)S(1)}, u32[]{:S(2)}) copy-start(f32[256]{0:T(256)S(1)} %mul.759) | copy-start | bytes 3076
  110.0 7.8 %copy-start.31 = (pred[128,1024]{0,1:T(8,128)(4,1)}, pred[128,1024]{0,1:T(8,128)(4,1)S(1)}, u32[]{:S(2)}) copy-start(pred[128,1024]{0,1:T(8,128)(4,1)S(1)} %iota_compare_fusion) | copy-start | bytes 393220
  120.4 346.2 %reduce-scatter.10.cloned.1.call-start = ((), (), s32[]{:S(2)}) async-start(), calls=%async_computation.7 | async-start | bytes 2580480
  125.9 21.6 %copy-start.55 = (f32[128]{0:T(128)}, f32[128]{0:T(128)S(1)}, u32[]{:S(2)}) copy-start(f32[128]{0:T(128)S(1)} %get-tuple-element.170) | copy-start | bytes 1540
  126.0 21.5 %copy-start.39 = (f32[1152]{0:T(1024)}, f32[1152]{0:T(1024)S(1)}, u32[]{:S(2)}) copy-start(f32[1152]{0:T(1024)S(1)} %mul.781) | copy-start | bytes 13828
  127.8 26.9 %copy-start.59 = (f32[128]{0:T(128)}, f32[128]{0:T(128)S(1)}, u32[]{:S(2)}) copy-start(f32[128]{0:T(128)S(1)} %get-tuple-element.172) | copy-start | bytes 1540
  241.3 6.6 %copy-start.17 = (bf16[8,128,1152]{2,1,0:T(8,128)(2,1)S(1)}, bf16[8,128,1152]{2,1,0:T(8,128)(2,1)}, u32[]{:S(2)}) copy-start(bf16[8,128,1152]{2,1,0:T(8,128)(2,1)} %exchange_4.1) | copy-start | bytes 7077892
  241.3 6.5 %copy-start.72 = (bf16[1152,864]{1,0:T(8,128)(2,1)S(1)}, bf16[1152,864]{1,0:T(8,128)(2,1)}, u32[]{:S(2)}) copy-start(bf16[1152,864]{1,0:T(8,128)(2,1)} %all-gather.9.cloned.1.call-done) | copy-start | bytes 5971972
  241.3 6.5 %copy-start.75 = (f32[1024,864]{0,1:T(8,128)S(1)}, f32[1024,864]{0,1:T(8,128)}, u32[]{:S(2)}) copy-start(f32[1024,864]{0,1:T(8,128)} %fusion.95) | copy-start | bytes 10616836
  241.3 6.5 %copy-start.76 = (f32[1024,864]{0,1:T(8,128)S(1)}, f32[1024,864]{0,1:T(8,128)}, u32[]{:S(2)}) copy-start(f32[1024,864]{0,1:T(8,128)} %get-tuple-element.184) | copy-start | bytes 10616836
  271.7 197.5 %reduce-scatter.12.cloned.1.call-start = ((), (), s32[]{:S(2)}) async-start(), calls=%async_computation.8 | async-start | bytes 2580480
  312.7 159.1 %reduce-scatter.14.cloned.1.call-start = ((), (), s32[]{:S(2)}) async-start(), calls=%async_computation.9 | async-start | bytes 2580480
  330.4 19.3 %copy-start.28 = (f32[128,128]{1,0:T(8,128)S(1)}, f32[128,128]{1,0:T(8,128)}, u32[]{:S(2)}) copy-start(f32[128,128]{1,0:T(8,128)} %copy-done.27) | copy-start | bytes 196612
  330.4 19.4 %copy-start.8 = (f32[128,4,256]{2,0,1:T(8,128)S(1)}, f32[128,4,256]{2,0,1:T(8,128)}, u32[]{:S(2)}) copy-start(f32[128,4,256]{2,0,1:T(8,128)} %copy-done.7) | copy-start | bytes 1572868
  330.4 19.4 %copy-start.43 = (f32[128,4]{0,1:T(4,128)S(1)}, f32[128,4]{0,1:T(4,128)}, u32[]{:S(2)}) copy-start(f32[128,4]{0,1:T(4,128)} %copy-done.42) | copy-start | bytes 6148
  364.0 19.7 %copy-start.6 = (bf16[8,128,1152]{2,1,0:T(8,128)(2,1)S(1)}, bf16[8,128,1152]{2,1,0:T(8,128)(2,1)}, u32[]{:S(2)}) copy-start(bf16[8,128,1152]{2,1,0:T(8,128)(2,1)} %get-tuple-element.48) | copy-start | bytes 7077892
  364.1 19.7 %copy-start.63 = (f32[8,128]{1,0:T(8,128)S(1)}, f32[8,128]{1,0:T(8,128)}, u32[]{:S(2)}) copy-start(f32[8,128]{1,0:T(8,128)} %get-tuple-element.159) | copy-start | bytes 12292
  459.6 5.9 %copy-start.69 = (f32[128]{0:T(128)S(1)}, f32[128]{0:T(128)}, u32[]{:S(2)}) copy-start(f32[128]{0:T(128)} %get-tuple-element.165) | copy-start | bytes 1540
  (60 other events, 177.2 us)
Sparse Core Ops, SparseCore 0:
  38.9 45.2 all-gather.4
  85.8 43.9 all-gather.6
  131.3 43.9 all-gather.8
  177.6 43.8 all-gather.10
  271.8 40.3 reduce-scatter.9
  314.3 42.2 reduce-scatter.11
  359.0 47.1 reduce-scatter.13
where the time goes:
time: 490 us; the launch traced here: 481 us
  Pallas kernels  258 us (53%)
  local copies, waits for them, and re-layouts  72.7 us (15%)
  matrix products  71.7 us (15%)
  other arithmetic  49.8 us (10%)
  between operations  15.4 us (3%)
  waiting for transfers between devices  13 us (3%)
    pallas_call x10, Pallas kernels, exchange(): pl.pallas_call(functools.partial(body, size, axis, tuple(kinds)), out_sha...  258 us
    unnamed x165, local copies, waits for them, and re-layouts  32.1 us
    dot_general x8, matrix products, matmul(): return jnp.dot(left, right, preferred_element_type=jnp.float32)  28.3 us
    dot_general x5, matrix products, matmul_tn(): lax.dot_general(left, right, (((0,), (0,)), ((), ())), preferred_element_...  19.3 us
    dot_general x6, matrix products, matmul_nt(): lax.dot_general(left, right, (((1,), (1,)), ((), ())), preferred_element_...  15.7 us
    all_gather x1, waiting for transfers between devices, on_device(): lax.all_gather(down_weight, 'dp', axis=0, tiled=True)  11.5 us
    reduce_sum x8, other arithmetic, sum_blocks(): return jnp.sum(array.astype(jnp.float32), axis=0)  11.4 us
  transfers between devices with their start and end apart: 7, of which 1 were waited for; matrix products, arithmetic and copies ran while one was open for 30% of the time, Pallas kernels for 49%

commit v1 on v0

--- a/solution.py
+++ b/solution.py
@@ -232,6 +232,540 @@
     )(*arrays)
 
 
+def pieces_of(rows):
+    parts = chunks_of(rows)
+    return [pl.ds(part * (rows // parts), rows // parts) for part in range(parts)]
+
+
+def remote(source, target, send, recv, axis, peer):
+    copy = pltpu.make_async_remote_copy(
+        src_ref=source,
+        dst_ref=target,
+        send_sem=send,
+        recv_sem=recv,
+        device_id={axis: peer},
+        device_id_type=MESH,
+    )
+    copy.start()
+    return copy
+
+
+class Place:
+    def __init__(self, axis, size):
+        self.axis, self.size, self.half = axis, size, size // 2
+        self.me = lax.axis_index(axis)
+        self.core = lax.rem(self.me, 2)
+        self.twin = self.me + 1 - 2 * self.core
+
+    def across(self, step):
+        return lax.rem(self.me + 2 * step, self.size)
+
+    def behind(self, step):
+        return lax.rem(self.me + self.size - 2 * step, self.size)
+
+    def greet_pairs(self):
+        barrier = pltpu.get_barrier_semaphore()
+        for step in range(1, self.half):
+            pl.semaphore_signal(
+                barrier, inc=1, device_id={self.axis: self.across(step)}, device_id_type=MESH
+            )
+        pl.semaphore_signal(barrier, inc=1, device_id={self.axis: self.twin}, device_id_type=MESH)
+        pl.semaphore_wait(barrier, self.half)
+
+    def greet_all(self):
+        barrier = pltpu.get_barrier_semaphore()
+        for step in range(1, self.size):
+            peer = lax.rem(self.me + step, self.size)
+            pl.semaphore_signal(barrier, inc=1, device_id={self.axis: peer}, device_id_type=MESH)
+        pl.semaphore_wait(barrier, self.size - 1)
+
+
+def scatter_scratch(size, rows, width):
+    half, parts, dma = size // 2, chunks_of(rows), pltpu.SemaphoreType.DMA
+    block = lambda count: pltpu.VMEM((count, rows, width), jnp.bfloat16)
+    return [block(half), block(half), block(half - 1), block(half - 1), dma((half,))] + [
+        dma((half, parts))
+    ] * 4
+
+
+class Scatter:
+    def __init__(self, place, part, scratch):
+        self.place, self.part = place, part
+        self.kept, self.twins, self.summed, self.landed = scratch[:4]
+        self.local, self.twin_send, self.twin_recv, self.send, self.recv = scratch[4:]
+        self.spans = pieces_of(self.kept.shape[1])
+
+    def load(self):
+        place = self.place
+        self.loads = []
+        for slot in range(place.half):
+            copy = pltpu.make_async_copy(
+                self.part.at[place.across(slot)], self.kept.at[slot], self.local.at[slot]
+            )
+            copy.start()
+            self.loads.append(copy)
+
+    def start(self):
+        place = self.place
+        self.twin_copies, self.copies = {}, {}
+        slots = list(range(1, place.half)) + [0]
+        for index, span in enumerate(self.spans):
+            for slot in slots:
+                self.twin_copies[slot, index] = remote(
+                    self.part.at[place.across(slot) + 1 - 2 * place.core, span],
+                    self.twins.at[slot, span],
+                    self.twin_send.at[slot, index],
+                    self.twin_recv.at[slot, index],
+                    place.axis,
+                    place.twin,
+                )
+        for copy in self.loads:
+            copy.wait()
+        for index, span in enumerate(self.spans):
+            for slot in slots[:-1]:
+                self.twin_copies[slot, index].wait_recv()
+                self.summed[slot - 1, span] = (
+                    self.kept[slot, span].astype(jnp.float32)
+                    + self.twins[slot, span].astype(jnp.float32)
+                ).astype(jnp.bfloat16)
+                self.copies[slot, index] = remote(
+                    self.summed.at[slot - 1, span],
+                    self.landed.at[slot - 1, span],
+                    self.send.at[slot, index],
+                    self.recv.at[slot, index],
+                    place.axis,
+                    place.across(slot),
+                )
+
+    def total(self, index):
+        span = self.spans[index]
+        self.twin_copies[0, index].wait_recv()
+        value = self.kept[0, span].astype(jnp.float32) + self.twins[0, span].astype(jnp.float32)
+        for slot in range(1, self.place.half):
+            self.copies[slot, index].wait_recv()
+            value = value + self.landed[slot - 1, span].astype(jnp.float32)
+        return value
+
+    def finish(self):
+        for copy in list(self.twin_copies.values()) + list(self.copies.values()):
+            copy.wait_send()
+
+
+def gather_scratch(size, rows):
+    dma = pltpu.SemaphoreType.DMA
+    return [dma((size // 2, chunks_of(rows)))] * 4 + [dma((chunks_of(rows),))]
+
+
+class Gather:
+    def __init__(self, place, source, target, scratch):
+        self.place, self.source, self.target = place, source, target
+        self.send, self.recv, self.pass_send, self.pass_recv, self.local = scratch
+        self.spans = pieces_of(source.shape[0])
+        self.across, self.last = [], []
+
+    def start(self, index):
+        place, span = self.place, self.spans[index]
+        for step in range(1, place.half):
+            copy = remote(
+                self.source.at[span],
+                self.target.at[place.me, span],
+                self.send.at[step, index],
+                self.recv.at[step, index],
+                place.axis,
+                place.across(step),
+            )
+            self.across.append((copy, step, index))
+        self.last.append(
+            remote(
+                self.source.at[span],
+                self.target.at[place.me, span],
+                self.pass_send.at[0, index],
+                self.pass_recv.at[0, index],
+                place.axis,
+                place.twin,
+            )
+        )
+        copy = pltpu.make_async_copy(
+            self.source.at[span], self.target.at[place.me, span], self.local.at[index]
+        )
+        copy.start()
+        self.last.append(copy)
+
+    def relay(self):
+        place = self.place
+        for copy, step, index in self.across:
+            copy.wait_recv()
+            block = self.target.at[place.behind(step), self.spans[index]]
+            self.last.append(
+                remote(
+                    block,
+                    block,
+                    self.pass_send.at[step, index],
+                    self.pass_recv.at[step, index],
+                    place.axis,
+                    place.twin,
+                )
+            )
+
+    def finish(self):
+        for copy, *_ in self.across:
+            copy.wait_send()
+        for copy in self.last:
+            copy.wait()
+
+
+def ffn_turn_kernel(axis, size, part, residual, cot, gain, block_out, gain_grad, gathered, grad, *scratch):
+    place = Place(axis, size)
+    scatter = Scatter(place, part, scratch[:9])
+    gather = Gather(place, grad, gathered, scratch[9:])
+    scatter.load()
+    place.greet_pairs()
+    scatter.start()
+    gain_row = gain[...]
+    for index, span in enumerate(scatter.spans):
+        ffn_sum = scatter.total(index)
+        inverse = inverse_rms(ffn_sum)
+        incoming = cot[span].astype(jnp.float32)
+        grad[span] = norm_back(ffn_sum, inverse, gain_row, incoming).astype(jnp.bfloat16)
+        gather.start(index)
+        scaled = ffn_sum * inverse
+        block_out[span] = (residual[span] + scaled * gain_row).astype(jnp.bfloat16)
+        share = jnp.sum(incoming * scaled, axis=0, keepdims=True)
+        gain_grad[...] = share if index == 0 else gain_grad[...] + share
+    gather.relay()
+    scatter.finish()
+    gather.finish()
+
+
+def ffn_turn(part, residual, cotangent, gain, axis, size, ident):
+    rows, width = residual.shape
+    whole = pl.BlockSpec(memory_space=pltpu.VMEM)
+    away = pl.BlockSpec(memory_space=pl.ANY)
+    return pl.pallas_call(
+        functools.partial(ffn_turn_kernel, axis, size),
+        out_shape=(
+            jax.ShapeDtypeStruct((rows, width), jnp.bfloat16),
+            jax.ShapeDtypeStruct((1, width), jnp.float32),
+            jax.ShapeDtypeStruct((size, rows, width), jnp.bfloat16),
+        ),
+        in_specs=[away, whole, whole, whole],
+        out_specs=(whole, whole, away),
+        scratch_shapes=[pltpu.VMEM((rows, width), jnp.bfloat16)]
+        + scatter_scratch(size, rows, width)
+        + gather_scratch(size, rows),
+        compiler_params=pltpu.CompilerParams(collective_id=ident, has_side_effects=True),
+        cost_estimate=pl.CostEstimate(
+            flops=0, bytes_accessed=20 * part.size * 2, transcendentals=0
+        ),
+        name=f"ffn_turn_{ident}",
+    )(part, residual, cotangent, gain)
+
+
+def attn_back_kernel(
+    axis,
+    size,
+    part,
+    residual,
+    cot,
+    projected,
+    tokens,
+    gains,
+    head_gains,
+    out_hbm,
+    query_hbm,
+    pair_hbm,
+    attn_out,
+    query_rot,
+    key_hbm,
+    value_hbm,
+    queries,
+    keys,
+    cosine,
+    sine,
+    post_grad,
+    input_grad,
+    query_cols,
+    pair_cols,
+    proj_cols,
+    all_gains,
+    out_w,
+    query_w,
+    pair_w,
+    key_all,
+    value_all,
+    res_grad,
+    proj_grad,
+    stacked_p,
+    stacked_s,
+    stacked_g,
+    stacked_q,
+    pair_part,
+    query_grad,
+    query_send,
+    pair_send,
+    proj_send,
+    gain_send,
+    local,
+    send,
+    recv,
+    *scratch,
+):
+    rows, width = residual.shape
+    total_keys = key_all.shape[0]
+    bf16, f32 = jnp.bfloat16, jnp.float32
+    scaling = 1.0 / math.sqrt(HEAD)
+    place = Place(axis, size)
+    me = place.me
+    two = Scatter(place, part, scratch[:9])
+    pairs = Scatter(place, pair_part, scratch[9:])
+    two.load()
+    loads = []
+    for source, target in (
+        (out_hbm, out_w),
+        (key_hbm, key_all),
+        (value_hbm, value_all),
+        (query_hbm, query_w),
+        (pair_hbm, pair_w),
+    ):
+        copy = pltpu.make_async_copy(source, target, local.at[len(loads)])
+        copy.start()
+        loads.append(copy)
+    place.greet_all()
+    two.start()
+    swaps = []
+
+    def swap(item, source, target):
+        for step in range(1, size):
+            peer = lax.rem(me + step, size)
+            swaps.append(
+                remote(
+                    source.at[peer],
+                    target.at[me],
+                    send.at[item, step - 1],
+                    recv.at[item, step - 1],
+                    axis,
+                    peer,
+                )
+            )
+        copy = pltpu.make_async_copy(source.at[me], target.at[me], local.at[len(loads) + item])
+        copy.start()
+        swaps.append(copy)
+
+    gain_in, gain_attn, gain_pre = gains[0:1], gains[1:2], gains[2:3]
+    gain_query, gain_key = head_gains[0:1], head_gains[1:2]
+    gain_send[...] = jnp.zeros_like(gain_send)
+    gain_send[3:4] = post_grad[...]
+    proj_width = width // size
+    for index, span in enumerate(two.spans):
+        two_grad = two.total(index)
+        kept = residual[span]
+        inv_two = inverse_rms(kept)
+        back = cot[span].astype(f32) + norm_back(kept, inv_two, gain_pre, two_grad)
+        res_grad[span] = back
+        ahead = projected[span]
+        inv_proj = inverse_rms(ahead)
+        proj_back = norm_back(ahead, inv_proj, gain_attn, back)
+        proj_grad[span] = proj_back.astype(bf16)
+        for peer in range(size):
+            proj_send[peer, span] = proj_back[:, peer * proj_width : (peer + 1) * proj_width].astype(
+                bf16
+            )
+        gain_send[2:3] += jnp.sum(two_grad * kept * inv_two, axis=0, keepdims=True)
+        gain_send[1:2] += jnp.sum(back * ahead * inv_proj, axis=0, keepdims=True)
+    swap(0, proj_send, proj_cols)
+    loads[0].wait()
+    attn_grad = matmul_nt(proj_grad[...], out_w[...]).astype(bf16)
+    loads[1].wait()
+    loads[2].wait()
+    query_pos = me * rows + lax.broadcasted_iota(jnp.int32, (rows, total_keys), 0)
+    allowed = query_pos >= lax.broadcasted_iota(jnp.int32, (rows, total_keys), 1)
+    for head in range(HEADS):
+        lanes = slice(head * HEAD, (head + 1) * HEAD)
+        level = pl.ds(head * rows, rows)
+        query = query_rot[:, lanes]
+        incoming = attn_grad[:, lanes]
+        scores = jnp.where(allowed, matmul_nt(query, key_all[...]), NEG_FILL)
+        weights = jnp.where(
+            allowed, jnp.exp(scores - jnp.max(scores, axis=-1, keepdims=True)), 0.0
+        )
+        probs = weights / jnp.sum(weights, axis=-1, keepdims=True)
+        delta = jnp.sum(
+            incoming.astype(f32) * attn_out[:, lanes].astype(f32), axis=-1, keepdims=True
+        )
+        prob_grad = matmul_nt(incoming, value_all[...])
+        stacked_s[level] = (probs * (prob_grad - delta)).astype(bf16)
+        stacked_p[level] = probs.astype(bf16)
+        stacked_g[level] = incoming
+        stacked_q[level] = query
+    values_part = matmul_tn(stacked_p[...], stacked_g[...]).astype(bf16)
+    keys_part = matmul_tn(stacked_s[...], stacked_q[...]).astype(bf16)
+    for peer in range(size):
+        block = slice(peer * rows, (peer + 1) * rows)
+        pair_part[peer, :, :HEAD] = keys_part[block]
+        pair_part[peer, :, HEAD:] = values_part[block]
+    pairs.load()
+    pairs.start()
+    query_width = HEADS * HEAD // size
+    gain_share = jnp.zeros((1, HEAD), f32)
+    for head in range(HEADS):
+        lanes = slice(head * HEAD, (head + 1) * HEAD)
+        level = pl.ds(head * rows, rows)
+        normed_grad = unrotate(
+            matmul(stacked_s[level], key_all[...]) * scaling, cosine[...], sine[...]
+        )
+        value = queries[:, lanes]
+        inverse = inverse_rms(value)
+        gain_share = gain_share + jnp.sum(normed_grad * value * inverse, axis=0, keepdims=True)
+        query_grad[:, lanes] = norm_back(value, inverse, gain_query, normed_grad).astype(bf16)
+    for peer in range(size):
+        query_send[peer] = query_grad[:, peer * query_width : (peer + 1) * query_width]
+    swap(1, query_send, query_cols)
+    gain_send[4:5, :HEAD] = gain_share
+    loads[3].wait()
+    input_grad[...] = matmul_nt(query_grad[...], query_w[...])
+    loads[4].wait()
+    pair_width = 2 * HEAD // size
+    key_share = jnp.zeros((1, HEAD), f32)
+    for index, span in enumerate(pairs.spans):
+        pair_total = pairs.total(index)
+        normed_grad = unrotate(pair_total[:, :HEAD], cosine[span], sine[span])
+        value = keys[span]
+        inverse = inverse_rms(value)
+        key_share = key_share + jnp.sum(normed_grad * value * inverse, axis=0, keepdims=True)
+        both = jnp.concatenate(
+            [norm_back(value, inverse, gain_key, normed_grad), pair_total[:, HEAD:]], axis=1
+        )
+        for peer in range(size):
+            pair_send[peer, span] = both[:, peer * pair_width : (peer + 1) * pair_width].astype(bf16)
+        one_grad = input_grad[span] + matmul_nt(both.astype(bf16), pair_w[...])
+        inputs = tokens[span].astype(f32)
+        inv_one = inverse_rms(inputs)
+        gain_send[0:1] += jnp.sum(one_grad * inputs * inv_one, axis=0, keepdims=True)
+        input_grad[span] = res_grad[span] + norm_back(inputs, inv_one, gain_in, one_grad)
+    gain_send[5:6, :HEAD] = key_share
+    swap(2, pair_send, pair_cols)
+    for step in range(1, size):
+        peer = lax.rem(me + step, size)
+        swaps.append(
+            remote(
+                gain_send,
+                all_gains.at[me],
+                send.at[3, step - 1],
+                recv.at[3, step - 1],
+                axis,
+                peer,
+            )
+        )
+    copy = pltpu.make_async_copy(gain_send, all_gains.at[me], local.at[len(loads) + 3])
+    copy.start()
+    swaps.append(copy)
+    two.finish()
+    pairs.finish()
+    for copy in swaps:
+        copy.wait()
+
+
+def attn_back(
+    part,
+    residual,
+    cotangent,
+    projected,
+    tokens,
+    gains,
+    head_gains,
+    out_full,
+    query_full,
+    pair_full,
+    attn_out,
+    query_rot,
+    key_all,
+    value_all,
+    queries,
+    keys,
+    cosine,
+    sine,
+    post_grad,
+    axis,
+    size,
+    ident,
+):
+    rows, width = residual.shape
+    bf16, f32 = jnp.bfloat16, jnp.float32
+    whole = pl.BlockSpec(memory_space=pltpu.VMEM)
+    away = pl.BlockSpec(memory_space=pl.ANY)
+    qwidth, total_keys = query_full.shape[1], key_all.shape[0]
+    query_cols = (size, rows, qwidth // size)
+    pair_cols = (size, rows, 2 * HEAD // size)
+    proj_cols = (size, rows, width // size)
+    dma = pltpu.SemaphoreType.DMA
+    return pl.pallas_call(
+        functools.partial(attn_back_kernel, axis, size),
+        out_shape=(
+            jax.ShapeDtypeStruct((rows, width), f32),
+            jax.ShapeDtypeStruct(query_cols, bf16),
+            jax.ShapeDtypeStruct(pair_cols, bf16),
+            jax.ShapeDtypeStruct(proj_cols, bf16),
+            jax.ShapeDtypeStruct((size, 8, width), f32),
+        ),
+        in_specs=[away]
+        + [whole] * 6
+        + [away] * 3
+        + [whole] * 2
+        + [away] * 2
+        + [whole] * 5,
+        out_specs=(whole, away, away, away, away),
+        scratch_shapes=[
+            pltpu.VMEM(out_full.shape, bf16),
+            pltpu.VMEM(query_full.shape, bf16),
+            pltpu.VMEM(pair_full.shape, bf16),
+            pltpu.VMEM(key_all.shape, bf16),
+            pltpu.VMEM(value_all.shape, bf16),
+            pltpu.VMEM((rows, width), f32),
+            pltpu.VMEM((rows, width), bf16),
+            pltpu.VMEM((HEADS * rows, total_keys), bf16),
+            pltpu.VMEM((HEADS * rows, total_keys), bf16),
+            pltpu.VMEM((HEADS * rows, HEAD), bf16),
+            pltpu.VMEM((HEADS * rows, HEAD), bf16),
+            pltpu.VMEM((size, rows, 2 * HEAD), bf16),
+            pltpu.VMEM((rows, qwidth), bf16),
+            pltpu.VMEM(query_cols, bf16),
+            pltpu.VMEM(pair_cols, bf16),
+            pltpu.VMEM(proj_cols, bf16),
+            pltpu.VMEM((8, width), f32),
+            dma((9,)),
+            dma((4, size - 1)),
+            dma((4, size - 1)),
+        ]
+        + scatter_scratch(size, rows, width)
+        + scatter_scratch(size, rows, 2 * HEAD),
+        compiler_params=pltpu.CompilerParams(collective_id=ident, has_side_effects=True),
+        cost_estimate=pl.CostEstimate(
+            flops=0, bytes_accessed=30 * part.size * 2, transcendentals=0
+        ),
+        name=f"attn_back_{ident}",
+    )(
+        part,
+        residual,
+        cotangent,
+        projected,
+        tokens,
+        gains,
+        head_gains,
+        out_full,
+        query_full,
+        pair_full,
+        attn_out,
+        query_rot,
+        key_all,
+        value_all,
+        queries,
+        keys,
+        cosine,
+        sine,
+        post_grad,
+    )
+
+
 def by_columns(array, parts):
     rows, columns = array.shape
     return jnp.transpose(array.reshape(rows, parts, columns // parts), (1, 0, 2))
@@ -274,7 +808,6 @@
 
     qwidth = query_weight.shape[1]
     kwidth = key_weight.shape[1]
-    mixed_columns = (qwidth + 2 * kwidth) // ctx
     out_columns = out_weight.shape[1] // ctx
     query_columns = qwidth // ctx
     pair = jnp.concatenate([key_weight, value_weight], axis=1)
@@ -290,9 +823,6 @@
     packed_gains = jnp.concatenate([gain.astype(jnp.float32) for gain in gains])[None]
     query_dp, pair_dp, out_dp, gains_dp = exchange(
         (query_slice, pair_slice, out_slice, packed_gains), ("gather",) * 4, "dp", dp, 0
-    )
-    gate_weight, up_weight, down_weight, query_dp = lax.optimization_barrier(
-        (gate_weight, up_weight, down_weight, query_dp)
     )
     gate_full, up_full, down_full = (
         lax.all_gather(gate_weight, "dp", axis=0, tiled=True),
@@ -344,7 +874,6 @@
     accum = jnp.einsum(
         "hqk,kd->hqd", weights.astype(bf16), value_all, preferred_element_type=jnp.float32
     )
-    log_total = row_max + jnp.log(total)
     attn_heads = jnp.transpose(accum / total, (1, 0, 2)).astype(bf16)
     attn_out = attn_heads.reshape(rows, HEADS * HEAD)
     projected = matmul(attn_out, out_full)
@@ -353,24 +882,18 @@
     inv_two = inverse_rms(residual)
     normed_two = (residual * inv_two * gain_pre).astype(bf16)
 
-    attn_all = lax.all_gather(attn_out, "ctx", axis=0, tiled=True)
-    (rows_all,) = exchange((normed_two,), ("gather",), "ctx", ctx, 2)
+    rows_all, attn_all = exchange((normed_two, attn_out), ("gather",) * 2, "ctx", ctx, 2)
+    attn_all = attn_all.reshape(-1, attn_out.shape[1])
     rows_all = rows_all.reshape(-1, width)
     gate = matmul(rows_all, gate_full)
     upper = matmul(rows_all, up_full)
     gelu_val, gelu_der = gelu_pair(gate)
     hidden = (gelu_val * upper).astype(bf16)
     ffn_part = matmul_nt(hidden, down_full).astype(bf16).reshape(ctx, rows, width)
-    (ffn_parts,) = exchange((ffn_part,), ("swap",), "ctx", ctx, 3)
-    ffn_sum = sum_blocks(ffn_parts)
-    inv_ffn = inverse_rms(ffn_sum)
-    block_out = (residual + ffn_sum * inv_ffn * gain_post).astype(bf16)
-    cot = cotangent.astype(jnp.float32)
-    grad_post = jnp.sum(cot * ffn_sum * inv_ffn, axis=0)
-    ffn_sum_grad = norm_back(ffn_sum, inv_ffn, gain_post, cot).astype(bf16)
-
-    (grad_all,) = exchange((ffn_sum_grad,), ("gather",), "ctx", ctx, 4)
-    grad_all, attn_all = lax.optimization_barrier((grad_all.reshape(-1, width), attn_all))
+    block_out, grad_post, grad_all = ffn_turn(
+        ffn_part, residual, cotangent, gain_post[None], "ctx", ctx, 3
+    )
+    grad_all = grad_all.reshape(-1, width)
     down_part, grad_all = lax.optimization_barrier(
         (matmul_tn(grad_all, hidden).astype(bf16), grad_all)
     )
@@ -390,97 +913,74 @@
     gate_shard = gate_shard.astype(jnp.float32)
     up_shard = lax.psum_scatter(up_part, "dp", scatter_dimension=0, tiled=True)
     up_shard = up_shard.astype(jnp.float32)
-    (two_parts,) = exchange((two_part.reshape(ctx, rows, width),), ("swap",), "ctx", ctx, 5)
-    normed_two_grad = sum_blocks(two_parts)
-    grad_pre = jnp.sum(normed_two_grad * residual * inv_two, axis=0)
-    residual_grad = cot + norm_back(residual, inv_two, gain_pre, normed_two_grad)
-    grad_attn = jnp.sum(residual_grad * projected * inv_proj, axis=0)
-    projected_grad = norm_back(projected, inv_proj, gain_attn, residual_grad).astype(bf16)
-    attn_out_grad = matmul_nt(projected_grad, out_full).astype(bf16).reshape(rows, HEADS, HEAD)
-    delta = jnp.sum(attn_out_grad.astype(jnp.float32) * attn_heads.astype(jnp.float32), axis=-1)
-    delta = jnp.transpose(delta, (1, 0))[:, :, None]
-    probs = jnp.where(allowed, jnp.exp(scores - log_total), 0.0)
-    prob_grad = jnp.einsum(
-        "qhd,kd->hqk", attn_out_grad, value_all, preferred_element_type=jnp.float32
-    )
-    score_grad = (probs * (prob_grad - delta)).astype(bf16)
-    values_part = jnp.einsum(
-        "hqk,qhd->kd", probs.astype(bf16), attn_out_grad, preferred_element_type=jnp.float32
-    )
-    keys_part = jnp.einsum("hqk,qhd->kd", score_grad, query_rot, preferred_element_type=jnp.float32)
-    query_rot_grad = jnp.einsum(
-        "hqk,kd->qhd", score_grad, key_all, preferred_element_type=jnp.float32
-    )
-    keys_parts, values_parts = exchange(
-        (
-            keys_part.astype(bf16).reshape(ctx, rows, kwidth),
-            values_part.astype(bf16).reshape(ctx, rows, kwidth),
-        ),
-        ("swap", "swap"),
+    input_grad, query_cols, pair_cols, proj_cols, all_gains = attn_back(
+        two_part.reshape(ctx, rows, width),
+        residual,
+        cotangent,
+        projected,
+        tokens,
+        jnp.stack([gain_in, gain_attn, gain_pre]),
+        jnp.stack([gain_query, gain_key]),
+        out_full,
+        query_full,
+        pair_full,
+        attn_out,
+        query_rot.reshape(rows, HEADS * HEAD),
+        key_all,
+        value_all,
+        queries.reshape(rows, HEADS * HEAD),
+        keys,
+        cosine,
+        sine,
+        grad_post,
         "ctx",
         ctx,
-        6,
-    )
-    key_rot_grad = sum_blocks(keys_parts)
-    value_grad = sum_blocks(values_parts).astype(bf16)
-    query_normed_grad = unrotate(query_rot_grad * scaling, cosine[:, None, :], sine[:, None, :])
-    grad_qgain = jnp.sum(query_normed_grad * queries * inv_query, axis=(0, 1))
-    query_grad = (
-        norm_back(queries, inv_query, gain_query, query_normed_grad)
-        .reshape(rows, HEADS * HEAD)
-        .astype(bf16)
-    )
-    key_normed_grad = unrotate(key_rot_grad, cosine, sine)
-    grad_kgain = jnp.sum(key_normed_grad * keys * inv_key, axis=0)
-    key_grad = norm_back(keys, inv_key, gain_key, key_normed_grad).astype(bf16)
-    mixed_grad = jnp.concatenate([query_grad, key_grad, value_grad], axis=1)
-    normed_one_grad = matmul_nt(query_grad, query_full) + matmul_nt(
-        mixed_grad[:, qwidth:], pair_full
-    )
-    grad_in = jnp.sum(normed_one_grad * inputs_f * inv_one, axis=0)
-    input_grad = residual_grad + norm_back(inputs_f, inv_one, gain_in, normed_one_grad)
-
-    gain_grads = (grad_in, grad_qgain, grad_kgain, grad_attn, grad_pre, grad_post)
+        5,
+    )
+    gain_sums = jnp.sum(all_gains, axis=0)
+    gain_grads = (
+        gain_sums[0],
+        gain_sums[4, :HEAD],
+        gain_sums[5, :HEAD],
+        gain_sums[1],
+        gain_sums[2],
+        gain_sums[3],
+    )
     packed = jnp.concatenate([grad.reshape(dp, -1) for grad in gain_grads], axis=1)
-    both = jnp.concatenate([by_columns(mixed_grad, ctx), by_columns(projected_grad, ctx)], axis=2)
-    both, gain_parts = exchange(
-        (both, by_columns(packed, ctx)),
-        ("swap",) * 2,
-        "ctx",
-        ctx,
-        7,
-    )
-    mixed_w = matmul_tn(normed_all, both[:, :, :mixed_columns].reshape(-1, mixed_columns)).astype(bf16)
-    out_w = matmul_tn(attn_all, both[:, :, mixed_columns:].reshape(-1, out_columns)).astype(bf16)
-    mixed_w, out_w, gain_parts = exchange(
+    query_w = matmul_tn(normed_all, query_cols.reshape(-1, query_columns)).astype(bf16)
+    pair_w = matmul_tn(normed_all, pair_cols.reshape(normed_all.shape[0], -1)).astype(bf16)
+    out_w = matmul_tn(attn_all, proj_cols.reshape(-1, out_columns)).astype(bf16)
+    query_w, pair_w, out_w, gain_parts = exchange(
         (
-            mixed_w.reshape(dp, -1, mixed_columns),
+            query_w.reshape(dp, -1, query_columns),
+            pair_w.reshape(dp, -1, pair_w.shape[1]),
             out_w.reshape(dp, -1, out_columns),
-            sum_blocks(gain_parts)[:, None],
+            packed[:, None],
         ),
-        ("swap",) * 3,
+        ("swap",) * 4,
         "dp",
         dp,
         8,
     )
-    mixed_w, out_w, gain_parts = exchange(
-        (sum_blocks(mixed_w).astype(bf16), sum_blocks(out_w).astype(bf16), sum_blocks(gain_parts)),
+    query_w, pair_w, out_w = exchange(
+        (sum_blocks(query_w).astype(bf16), sum_blocks(pair_w).astype(bf16), sum_blocks(out_w).astype(bf16)),
         ("gather",) * 3,
         "ctx",
         ctx,
         9,
     )
-    mixed_w = from_columns(mixed_w).astype(jnp.float32)
+    query_w = from_columns(query_w).astype(jnp.float32)
+    pair_w = from_columns(pair_w).astype(jnp.float32)
     out_w = from_columns(out_w).astype(jnp.float32)
-    gain_done = gain_parts.reshape(-1)
+    gain_done = sum_blocks(gain_parts).reshape(-1)
     share = [gain_done[low:high] for low, high in zip(cuts[:-1], cuts[1:])]
     return (
         block_out,
         input_grad,
         share[0],
-        mixed_w[:, :qwidth],
-        mixed_w[:, qwidth : qwidth + kwidth],
-        mixed_w[:, qwidth + kwidth :],
+        query_w,
+        pair_w[:, :kwidth],
+        pair_w[:, kwidth:],
         share[1],
         share[2],
         out_w,

time: 490 us -> 437 us (0.89)
  other arithmetic: 49.8 us -> 24.5 us
  local copies, waits for them, and re-layouts: 72.7 us -> 56.6 us
  Pallas kernels: 258 us -> 269 us
  waiting for transfers between devices: 13 us -> 2.14 us
  matrix products: 71.7 us -> 63 us
    pallas_call x0 -> x2, Pallas kernels: none -> 81.1 us  [the longest x1 45.8 us: attn_back(): pl.pallas_call(functools.partial(attn_back_kernel, axis, size), out_shape...]
    pallas_call x10 -> x5, Pallas kernels: 258 us -> 187 us  [exchange(): pl.pallas_call(functools.partial(body, size, axis, tuple(kinds)), out_sha...]
    all_gather x1, waiting for transfers between devices: 11.5 us -> 0.01 us  [on_device(): lax.all_gather(down_weight, 'dp', axis=0, tiled=True)]
    dot_general x5 -> x0, matrix products: 7.64 us -> none  [the longest x1 2.58 us: on_device(): jnp.einsum('qhd,kd->hqk', attn_out_grad, value_all, preferred_element_typ...]
    convert_element_type x9 -> x4, local copies, waits for them, and re-layouts: 10.3 us -> 3.08 us  [the longest x1 1 us: on_device(): out_w = matmul_tn(attn_all, proj_cols.reshape(-1, out_columns)).astype(bf16)]
    reduce_sum x7 -> x1, other arithmetic: 7.22 us -> 0.99 us  [on_device(): gain_sums = jnp.sum(all_gains, axis=0)]
    reduce_sum x8 -> x4, other arithmetic: 11.4 us -> 5.94 us  [sum_blocks(): return jnp.sum(array.astype(jnp.float32), axis=0)]
    slice x3, local copies, waits for them, and re-layouts: 5.11 us -> 0.13 us  [the longest x1 0.05 us: on_device(): pair_w[:, kwidth:]]
  transfers between devices with their start and end apart: 7 -> 6, of which waited for: 1 -> 0; matrix products, arithmetic and copies ran while one was open for 30% -> 24% of each run, Pallas kernels for 49% -> 54%
where the time goes in v1:
time: 437 us; the launch traced here: 430 us
  Pallas kernels  269 us (62%)
  matrix products  63 us (14%)
  local copies, waits for them, and re-layouts  56.6 us (13%)
  other arithmetic  24.5 us (6%)
  between operations  15 us (3%)
    pallas_call x5, Pallas kernels, exchange(): pl.pallas_call(functools.partial(body, size, axis, tuple(kinds)), out_sha...  187 us
    pallas_call x1, Pallas kernels, attn_back(): pl.pallas_call(functools.partial(attn_back_kernel, axis, size), out_shape...  45.8 us
    pallas_call x1, Pallas kernels, ffn_turn(): pl.pallas_call(functools.partial(ffn_turn_kernel, axis, size), out_shape=...  35.3 us
    unnamed x101, local copies, waits for them, and re-layouts  27.7 us
    dot_general x8, matrix products, matmul(): return jnp.dot(left, right, preferred_element_type=jnp.float32)  25.9 us
    dot_general x6, matrix products, matmul_tn(): lax.dot_general(left, right, (((0,), (0,)), ((), ())), preferred_element_...  18.1 us
    dot_general x3, matrix products, matmul_nt(): lax.dot_general(left, right, (((1,), (1,)), ((), ())), preferred_element_...  13.9 us
  transfers between devices with their start and end apart: 6, of which 0 were waited for; matrix products, arithmetic and copies ran while one was open for 24% of the time, Pallas kernels for 54%

profile of v1, /device:TPU:0, one launch (start us, length us, event | category | flops | bytes accessed | tf_op | source)
XLA Modules:
  0.0 430.0 jit_solution(3472172490292407833)
XLA Ops:
  9.5 4.2 concatenate.18
  17.9 43.7 %exchange_0.1 = (bf16[4,288,128]{2,1,0:T(8,128)(2,1)}, bf16[4,36,512]{2,1,0:T(8,128)(2,1)}, bf16[4,32,1152]{2,1,0:T(8,128)(2,1)}, f32[4,1,1280]{2,1,0:T(1,128)}) custom-call(bf16[288,128]{1,0:T(8,128)(2,1)} %constant_dynamic-slice_fusion.1.refs_0_, bf16[36,512]{1,0:T(8,128)(2,1)} %fusion.48.refs_1_, bf16[32,1152]{1,0:T(8,128)(2,1)} %constant_dynamic-slice_fusion.refs_2_, ...), custom_call_target="tpu_custom_call" | custom-call | bytes 15155200 | tf_op jit(solution)/shard_map/exchange_0/pallas_call | solution.py:221
  62.7 52.7 %exchange_1.1 = (bf16[8,1152,128]{2,1,0:T(8,128)(2,1)}, bf16[8,4,36,512]{3,2,1,0:T(8,128)(2,1)}, bf16[8,4,32,1152]{3,2,1,0:T(8,128)(2,1)}, bf16[8,128,1152]{2,1,0:T(8,128)(2,1)}) custom-call(bf16[1152,128]{1,0:T(8,128)(2,1)} %bitcast.146, bf16[4,36,512]{2,1,0:T(8,128)(2,1)} %get-tuple-element.46.refs_1_, bf16[4,32,1152]{2,1,0:T(8,128)(2,1)} %get-tuple-element.47.refs_2_, ...), custom_call_target="tpu_custom_call" | custom-call | bytes 165150720 | tf_op jit(solution)/shard_map/exchange_1/pallas_call | solution.py:221
  115.4 2.7 copy.91
  118.1 2.9 reshape.269.pair_hbm
  138.5 3.3 fusion.29
  142.0 3.3 fusion.61
  149.0 30.6 %exchange_2.1 = (bf16[8,128,1152]{2,1,0:T(8,128)(2,1)}, bf16[8,128,1024]{2,1,0:T(8,128)(2,1)}) custom-call(bf16[128,1152]{1,0:T(8,128)(2,1)} %multiply_convert_fusion.5.refs_0_, bf16[128,1024]{1,0:T(8,128)(2,1)} %bitcast.136), custom_call_target="tpu_custom_call" | custom-call | bytes 89128960 | tf_op jit(solution)/shard_map/exchange_2/pallas_call | solution.py:221
  179.7 6.5 %fusion.66 = f32[1024,864]{0,1:T(8,128)} fusion(bf16[1024,1152]{1,0:T(8,128)(2,1)} %bitcast.150, bf16[1152,864]{1,0:T(8,128)(2,1)} %all-gather.4.cloned.1.call-done), kind=kOutput, calls=%fused_computation.123 | convolution fusion | flops 2038431744 | bytes 7888896 | tf_op jit(solution)/shard_map/dot_general | solution.py:68
  186.2 8.4 %multiply_convert_fusion.2 = (bf16[1024,864]{0,1:T(8,128)(2,1)S(1)}, f32[1024,864]{0,1:T(8,128)}) fusion(f32[1024,864]{0,1:T(8,128)} %fusion.66, bf16[1024,1152]{1,0:T(8,128)(2,1)} %bitcast.151, bf16[1152,864]{1,0:T(8,128)(2,1)} %all-gather.6.cloned.1.call-done), kind=kOutput, calls=%fused_computation.18 | convolution fusion | flops 2047279104 | bytes 13197312 | tf_op jit(solution)/shard_map/dot_general | solution.py:68
  194.7 6.6 %convolution_convert_fusion = bf16[1024,1152]{1,0:T(8,128)(2,1)} fusion(bf16[1024,864]{0,1:T(8,128)(2,1)S(1)} %get-tuple-element.173, bf16[1152,864]{1,0:T(8,128)(2,1)} %all-gather.8.cloned.1.call-done), kind=kOutput, calls=%fused_computation.9 | convolution fusion | flops 2039611392 | bytes 6119424 | tf_op jit(solution)/shard_map/dot_general | solution.py:78
  201.3 35.3 %ffn_turn_3.1 = (bf16[128,1152]{1,0:T(8,128)(2,1)}, f32[1,1152]{1,0:T(1,128)}, bf16[8,128,1152]{2,1,0:T(8,128)(2,1)}) custom-call(bf16[8,128,1152]{2,1,0:T(8,128)(2,1)} %bitcast.140, f32[128,1152]{1,0:T(8,128)} %copy-done.3, bf16[128,1152]{1,0:T(8,128)(2,1)} %cot.3, f32[1,1152]{1,0:T(1,128)} %broadcast_in_dim_reshape.17.gain), custom_call_target="tpu_custom_call" | custom-call | bytes 47185920 | tf_op jit(solution)/shard_map/ffn_turn_3/pallas_call | solution.py:444
  236.7 4.8 %convolution_convert_fusion.3 = bf16[1152,864]{0,1:T(8,128)(2,1)S(1)} fusion(bf16[1024,864]{0,1:T(8,128)(2,1)} %copy-done.42, bf16[1024,1152]{1,0:T(8,128)(2,1)} %bitcast.154), kind=kOutput, calls=%fused_computation.21 | convolution fusion | flops 2039427072 | bytes 6119424 | tf_op jit(solution)/shard_map/dot_general | solution.py:72
  242.2 5.3 %multiply_convert_fusion.1 = (bf16[1024,864]{0,1:T(8,128)(2,1)S(1)}, bf16[1024,864]{0,1:T(8,128)(2,1)S(1)}) fusion(f32[1024,864]{0,1:T(8,128)S(1)} %copy-done.40, f32[1024,864]{0,1:T(8,128)S(1)} %copy-done.41, bf16[1024,1152]{1,0:T(8,128)(2,1)S(1)} %bitcast.155, bf16[1152,864]{1,0:T(8,128)(2,1)S(1)} %copy-done.35), kind=kOutput, calls=%fused_computation.17 | convolution fusion | flops 2058780672 | bytes 14966784 | tf_op jit(solution)/shard_map/dot_general | solution.py:68
  247.5 3.7 convolution_convert_fusion.1
  251.2 3.8 convolution_convert_fusion.2
  255.0 2.9 fusion.67
  258.0 4.3 %add_convert_fusion = bf16[1024,1152]{1,0:T(8,128)(2,1)} fusion(f32[1024,1152]{1,0:T(8,128)S(1)} %fusion.67, bf16[1024,864]{0,1:T(8,128)(2,1)S(1)} %get-tuple-element.147, bf16[1152,864]{1,0:T(8,128)(2,1)S(1)} %copy-done.34), kind=kOutput, calls=%fused_computation.7 | convolution fusion | flops 2040791040 | bytes 10838016 | tf_op jit(solution)/shard_map/dot_general | solution.py:78
  262.3 4.1 copy.118
  266.4 4.1 copy.120
  279.8 45.8 %attn_back_5.1 = (f32[128,1152]{1,0:T(8,128)}, bf16[8,128,128]{2,1,0:T(8,128)(2,1)}, bf16[8,128,64]{2,1,0:T(8,128)(2,1)}, bf16[8,128,144]{2,1,0:T(8,128)(2,1)}, f32[8,8,1152]{2,1,0:T(8,128)}) custom-call(bf16[8,128,1152]{2,1,0:T(8,128)(2,1)} %bitcast.141, f32[128,1152]{1,0:T(8,128)} %copy-done.3, bf16[128,1152]{1,0:T(8,128)(2,1)} %cot.3, ...), custom_call_target="tpu_custom_call" | custom-call | bytes 70778880 | tf_op jit(solution)/shard_map/attn_back_5/pallas_call | solution.py:701
  335.7 41.5 %exchange_8.1 = (bf16[4,288,128]{2,1,0:T(8,128)(2,1)}, bf16[4,288,64]{2,1,0:T(8,128)(2,1)}, bf16[4,256,144]{2,1,0:T(8,128)(2,1)}, f32[4,1,1280]{2,1,0:T(1,128)}) custom-call(bf16[4,288,128]{2,1,0:T(8,128)(2,1)} %bitcast.147, bf16[4,288,64]{2,1,0:T(8,128)(2,1)} %bitcast.144, bf16[4,256,144]{2,1,0:T(8,128)(2,1)} %bitcast.142, ...), custom_call_target="tpu_custom_call" | custom-call | bytes 15155200 | tf_op jit(solution)/shard_map/exchange_8/pallas_call | solution.py:221
  383.2 18.8 %exchange_9.1 = (bf16[8,288,128]{2,1,0:T(8,128)(2,1)}, bf16[8,288,64]{2,1,0:T(8,128)(2,1)}, bf16[8,256,144]{2,1,0:T(8,128)(2,1)}) custom-call(bf16[288,128]{1,0:T(8,128)(2,1)} %reduce_sum.129.refs_0_, bf16[288,64]{1,0:T(8,128)(2,1)} %reduce_sum.130.refs_1_, bf16[256,144]{1,0:T(8,128)(2,1)} %reduce_sum.131.refs_2_), custom_call_target="tpu_custom_call" | custom-call | bytes 29491200 | tf_op jit(solution)/shard_map/exchange_9/pallas_call | solution.py:221
  408.4 2.7 copy.110
  (199 shorter events, 72.8 us)
Async XLA Ops:
  7.2 7.1 %copy-start = (bf16[288,1024]{1,0:T(8,128)(2,1)S(1)}, bf16[288,1024]{1,0:T(8,128)(2,1)}, u32[]{:S(2)}) copy-start(bf16[288,1024]{1,0:T(8,128)(2,1)} %param.17) | copy-start | bytes 1769476
  7.2 55.2 %copy-start.7 = (bf16[128,1152]{1,0:T(8,128)(2,1)S(1)}, bf16[128,1152]{1,0:T(8,128)(2,1)}, u32[]{:S(2)}) copy-start(bf16[128,1152]{1,0:T(8,128)(2,1)} %tokens.1) | copy-start | bytes 884740
  7.2 172.4 %all-gather.4.cloned.1.call-start = ((), (), s32[]{:S(2)}) async-start(), calls=%async_computation.3 | async-start | bytes 2580480 | tf_op jit(solution)/shard_map/all_gather | solution.py:828
  7.9 178.3 %all-gather.6.cloned.1.call-start = ((), (), s32[]{:S(2)}) async-start(), calls=%async_computation.4 | async-start | bytes 2580480 | tf_op jit(solution)/shard_map/all_gather | solution.py:829
  8.7 186.0 %all-gather.8.cloned.1.call-start = ((), (), s32[]{:S(2)}) async-start(), calls=%async_computation.5 | async-start | bytes 2580480 | tf_op jit(solution)/shard_map/all_gather | solution.py:830
  9.4 404.1 %reduce-scatter.10.cloned.1.call-start = ((), (), s32[]{:S(2)}) async-start(), calls=%async_computation.6 | async-start | bytes 2580480
  62.4 65.3 %copy-start.28 = (f32[4,64]{1,0:T(4,128)}, f32[4,64]{1,0:T(4,128)S(1)}, u32[]{:S(2)}) copy-start(f32[4,64]{1,0:T(4,128)S(1)} %get-tuple-element.159) | copy-start | bytes 3076
  62.4 65.4 %copy-start.26 = (f32[4,64]{1,0:T(4,128)}, f32[4,64]{1,0:T(4,128)S(1)}, u32[]{:S(2)}) copy-start(f32[4,64]{1,0:T(4,128)S(1)} %get-tuple-element.160) | copy-start | bytes 3076
  115.4 5.6 %copy-start.4 = (bf16[8,128,1152]{2,1,0:T(8,128)(2,1)S(1)}, bf16[8,128,1152]{2,1,0:T(8,128)(2,1)}, u32[]{:S(2)}) copy-start(bf16[8,128,1152]{2,1,0:T(8,128)(2,1)} %get-tuple-element.48) | copy-start | bytes 7077892
  130.7 16.5 %copy-start.2 = (bf16[4,8,32,1152]{3,2,1,0:T(8,128)(2,1)}, bf16[4,8,32,1152]{3,2,1,0:T(8,128)(2,1)S(1)}, u32[]{:S(2)}) copy-start(bf16[4,8,32,1152]{3,2,1,0:T(8,128)(2,1)S(1)} %copy.98) | copy-start | bytes 7077892
  131.7 10.0 %copy-start.9 = (f32[128,1024]{1,0:T(8,128)}, f32[128,1024]{1,0:T(8,128)S(1)}, u32[]{:S(2)}) copy-start(f32[128,1024]{1,0:T(8,128)S(1)} %fusion.46.queries) | copy-start | bytes 1572868
  137.0 4.9 %copy-start.21 = (f32[128,128]{1,0:T(8,128)}, f32[128,128]{1,0:T(8,128)S(1)}, u32[]{:S(2)}) copy-start(f32[128,128]{1,0:T(8,128)S(1)} %get-tuple-element.165.cosine) | copy-start | bytes 196612
  137.0 4.9 %copy-start.22 = (f32[128,128]{1,0:T(8,128)}, f32[128,128]{1,0:T(8,128)S(1)}, u32[]{:S(2)}) copy-start(f32[128,128]{1,0:T(8,128)S(1)} %get-tuple-element.166.sine) | copy-start | bytes 196612
  147.8 38.4 %copy-start.6 = (f32[128,1152]{1,0:T(8,128)}, f32[128,1152]{1,0:T(8,128)S(1)}, u32[]{:S(2)}) copy-start(f32[128,1152]{1,0:T(8,128)S(1)} %get-tuple-element.172.projected) | copy-start | bytes 1769476
  148.1 38.1 %copy-start.3 = (f32[128,1152]{1,0:T(8,128)}, f32[128,1152]{1,0:T(8,128)S(1)}, u32[]{:S(2)}) copy-start(f32[128,1152]{1,0:T(8,128)S(1)} %get-tuple-element.146.residual) | copy-start | bytes 1769476
  194.7 6.6 %copy-start.42 = (bf16[1024,864]{0,1:T(8,128)(2,1)}, bf16[1024,864]{0,1:T(8,128)(2,1)S(1)}, u32[]{:S(2)}) copy-start(bf16[1024,864]{0,1:T(8,128)(2,1)S(1)} %get-tuple-element.173) | copy-start | bytes 5308420
  236.6 5.6 %copy-start.41 = (f32[1024,864]{0,1:T(8,128)S(1)}, f32[1024,864]{0,1:T(8,128)}, u32[]{:S(2)}) copy-start(f32[1024,864]{0,1:T(8,128)} %get-tuple-element.174) | copy-start | bytes 10616836
  242.2 5.3 %copy-start.31 = (bf16[8,128,1152]{2,1,0:T(8,128)(2,1)S(1)}, bf16[8,128,1152]{2,1,0:T(8,128)(2,1)}, u32[]{:S(2)}) copy-start(bf16[8,128,1152]{2,1,0:T(8,128)(2,1)} %get-tuple-element.53) | copy-start | bytes 7077892
  266.4 149.7 %reduce-scatter.12.cloned.1.call-start = ((), (), s32[]{:S(2)}) async-start(), calls=%async_computation.7 | async-start | bytes 2580480
  270.6 148.2 %reduce-scatter.14.cloned.1.call-start = ((), (), s32[]{:S(2)}) async-start(), calls=%async_computation.8 | async-start | bytes 2580480
  279.8 48.2 %copy-start.5 = (bf16[8,128,1152]{2,1,0:T(8,128)(2,1)S(1)}, bf16[8,128,1152]{2,1,0:T(8,128)(2,1)}, u32[]{:S(2)}) copy-start(bf16[8,128,1152]{2,1,0:T(8,128)(2,1)} %get-tuple-element.48) | copy-start | bytes 7077892
  279.8 48.2 %copy-start.30 = (f32[8,128]{1,0:T(8,128)S(1)}, f32[8,128]{1,0:T(8,128)}, u32[]{:S(2)}) copy-start(f32[8,128]{1,0:T(8,128)} %get-tuple-element.163) | copy-start | bytes 12292
  406.8 5.5 %copy-start.23 = (bf16[8,288,128]{2,1,0:T(8,128)(2,1)S(1)}, bf16[8,288,128]{2,1,0:T(8,128)(2,1)}, u32[]{:S(2)}) copy-start(bf16[8,288,128]{2,1,0:T(8,128)(2,1)} %get-tuple-element.69) | copy-start | bytes 1769476
  417.5 5.4 %copy-start.1 = (bf16[288,1024]{1,0:T(8,128)(2,1)S(1)}, bf16[288,1024]{1,0:T(8,128)(2,1)}, u32[]{:S(2)}) copy-start(bf16[288,1024]{1,0:T(8,128)(2,1)} %param.17) | copy-start | bytes 1769476
  (25 other events, 77.2 us)
Sparse Core Ops, SparseCore 0:
  9.6 64.4 all-gather.3
  75.7 43.7 all-gather.5
  121.1 43.9 all-gather.7
  266.5 42.5 reduce-scatter.9
  311.3 56.0 reduce-scatter.11
  369.6 46.4 reduce-scatter.13
